TPU v7x, 128 devices: a whole 4x4x4 slice. The times are simulated.
128 devices in a mesh: energy: 8 (over y, core), layer: 16 (over x, z).
Axes of the slice: x: 4, y: 4, z: 4, core: 2. Of those that a mesh axis runs over, the one named last changes fastest.
Arguments:
- correlations: bfloat16 [128, 16, 4, 256, 256], P(('energy', 'layer')), may hold values from -6 to 6
- retarded: bfloat16 [128, 16, 2, 256, 256], P(('energy', 'layer')), may hold values from -0.15625 to 0.15625
- coupling: bfloat16 [16, 256, 256], P('layer'), may hold values from -0.375 to 0.375
- phonon_shifts: int32 [4], replicated, may hold values from 1 to 4, as said below
- phonon_coupling: float32 [4], replicated, may hold values from 0.3 to 1.2
- layer_orbitals: int32 [16], P('layer'), may hold values from 128 to 256, as said below
Outputs:
- left_correlations: bfloat16 [128, 16, 4, 256, 256], P('energy', 'layer')
Inputs may be any that keep to these rules, and one draw needn't show every extreme that they name: `phonon_shifts`: one of the offsets equals 4. `layer_orbitals`: some layer has all 256 orbitals live.
All inputs are finite; a program needn't handle non-finite values.
Results may differ from a plain program's by a relative error of at most 0.025.
Values may be sent and summed in bfloat16 or wider, within the bound.
No kernel may reach another device: no remote copies, remote signals or barrier semaphores. Data moves between devices by JAX's collectives and lax.ppermute only.
A program may use at most 128 MiB of HBM per device.

v0:
```python
import jax
import jax.numpy as jnp
from jax import lax
from jax.sharding import PartitionSpec as P

MODES = 4
SHIFT_MAX = 4
bose_ratio = 0.5


def with_halo(block, sides, width):
    for axis, dim in sides:
        count = lax.axis_size(axis)
        forward = [(i, i + 1) for i in range(count - 1)]
        backward = [(target, source) for source, target in forward]
        low = lax.ppermute(
            lax.slice_in_dim(block, block.shape[dim] - width, None, axis=dim), axis, forward
        )
        high = lax.ppermute(lax.slice_in_dim(block, 0, width, axis=dim), axis, backward)
        block = jnp.concatenate([low, block, high], axis=dim)
    return block


def mode_weights(shift_value):
    occupation = 1.0 / (jnp.exp(bose_ratio * shift_value.astype(jnp.float32)) - 1.0)
    lower_weight = jnp.stack([occupation, occupation, occupation + 1.0, occupation + 1.0])
    upper_weight = jnp.stack([occupation + 1.0, occupation + 1.0, occupation, occupation])
    return (lower_weight, upper_weight)


def left_product(matrix, stacked_block):
    return jnp.einsum(
        "...ab,...kbc->...kac", matrix, stacked_block, preferred_element_type=jnp.float32
    )


def right_product(stacked_block, matrix):
    return jnp.einsum(
        "...kab,...cb->...kac", stacked_block, matrix, preferred_element_type=jnp.float32
    )


def advance(previous, sigma_block, green_block, coupling_block):
    halfway = jnp.einsum(
        "...kab,cb->...kac", previous, coupling_block, preferred_element_type=jnp.float32
    ).astype(jnp.bfloat16)
    spread = jnp.einsum(
        "ab,...kbc->...kac", coupling_block, halfway, preferred_element_type=jnp.float32
    )
    source = (sigma_block.astype(jnp.float32) + spread).astype(jnp.bfloat16)
    green_real = green_block[..., 0, :, :]
    green_imag = green_block[..., 1, :, :]
    source_real = source[..., 0::2, :, :]
    source_imag = source[..., 1::2, :, :]
    inner_real = (
        left_product(green_real, source_real) - left_product(green_imag, source_imag)
    ).astype(jnp.bfloat16)
    inner_imag = (
        left_product(green_real, source_imag) + left_product(green_imag, source_real)
    ).astype(jnp.bfloat16)
    outer_real = right_product(inner_real, green_real) + right_product(inner_imag, green_imag)
    outer_imag = right_product(inner_imag, green_real) - right_product(inner_real, green_imag)
    stacked = jnp.stack([outer_real, outer_imag], axis=-3)
    return stacked.reshape(stacked.shape[:-4] + (4,) + stacked.shape[-2:]).astype(jnp.bfloat16)


def body(correlations, retarded, coupling, phonon_shifts, phonon_coupling, layer_orbitals):
    regrouped = lax.all_to_all(correlations, "layer", split_axis=1, concat_axis=0, tiled=True)
    energies_here = regrouped.shape[0]
    orbital_count = regrouped.shape[-1]
    padded = with_halo(regrouped, (("energy", 0),), SHIFT_MAX)
    accumulated = jnp.zeros(regrouped.shape, jnp.float32)
    for mode_index in range(MODES):
        shift_value = phonon_shifts[mode_index]
        lower_weight, upper_weight = mode_weights(shift_value)
        lower_block = lax.dynamic_slice_in_dim(padded, SHIFT_MAX - shift_value, energies_here, 0)
        upper_block = lax.dynamic_slice_in_dim(padded, SHIFT_MAX + shift_value, energies_here, 0)
        accumulated = accumulated + phonon_coupling[mode_index] * (
            lower_weight[:, None, None] * lower_block.astype(jnp.float32)
            + upper_weight[:, None, None] * upper_block.astype(jnp.float32)
        )
    orbital_index = jnp.arange(orbital_count, dtype=jnp.int32)
    live_count = layer_orbitals[:, None, None, None]
    live_mask = (orbital_index[:, None] < live_count) & (orbital_index[None, :] < live_count)
    sigma_blocks = jnp.where(live_mask, accumulated, 0.0).astype(jnp.bfloat16)
    returned = lax.all_to_all(sigma_blocks, "layer", split_axis=0, concat_axis=1, tiled=True)
    couplings = lax.all_gather(coupling, "layer", axis=0, tiled=True)
    layer_total = returned.shape[1]

    def layer_step(layer_index, state):
        previous, finished = state
        current = advance(
            previous,
            lax.dynamic_index_in_dim(returned, layer_index, 1, keepdims=False),
            lax.dynamic_index_in_dim(retarded, layer_index, 1, keepdims=False),
            lax.dynamic_index_in_dim(couplings, layer_index, 0, keepdims=False),
        )
        finished = lax.dynamic_update_index_in_dim(finished, current, layer_index, 1)
        return (current, finished)

    _, finished = lax.fori_loop(
        0, layer_total, layer_step, (correlations[:, 0], jnp.zeros_like(correlations))
    )
    return lax.all_to_all(finished, "layer", split_axis=1, concat_axis=0, tiled=True)


def solution(mesh):
    return jax.shard_map(
        body,
        mesh=mesh,
        in_specs=(
            P(("energy", "layer"), None, None, None, None),
            P(("energy", "layer"), None, None, None, None),
            P("layer", None, None),
            P(),
            P(),
            P("layer"),
        ),
        out_specs=P("energy", "layer", None, None, None),
        check_vma=False,
    )
```

profile of v0, /device:TPU:8, one launch (start us, length us, event | category | flops | bytes accessed | tf_op | source)
XLA Modules:
  0.0 559.1 jit_solution(11851508432102478930)
XLA Ops:
  6.5 12.2 %copy.25 = bf16[1,16,4,256,256]{3,4,2,0,1:T(8,128)(2,1)} copy(bf16[1,16,4,256,256]{4,3,2,1,0:T(8,128)(2,1)} %param.8) | data formatting | bytes 16777216 | tf_op args[0]
  18.8 104.3 %all_to_all.39 = bf16[1,16,4,256,256]{3,4,2,0,1:T(8,128)(2,1)S(1)} all-to-all(bf16[1,16,4,256,256]{3,4,2,0,1:T(8,128)(2,1)} %copy.25), channel_id=1, replica_groups=mesh['energy'=8,'layer'=16] {'layer'}, dimensions={1} | all-to-all | bytes 16777216 | tf_op jit(solution)/shard_map/all_to_all | solution.py:68
  124.7 2.4 copy-done
  128.6 1.9 collective-permute-start.1
  130.6 2.4 collective-permute-start
  148.3 6.1 %collective-permute-done.1 = bf16[4,1,4,256,256]{3,4,2,0,1:T(8,128)(2,1)S(1)} collective-permute-done((bf16[4,1,4,256,256]{3,4,2,0,1:T(8,128)(2,1)}, bf16[4,1,4,256,256]{3,4,2,0,1:T(8,128)(2,1)S(1)}, u32[]{:S(2)}, u32[]{:S(2)}) %collective-permute-start.1) | collective-permute-done | bytes 2097184 | tf_op jit(solution)/shard_map/ppermute | solution.py:19
  154.4 3.8 collective-permute-done
  158.2 6.4 %pad_maximum_fusion = bf16[24,1,4,256,256]{3,4,2,0,1:T(8,128)(2,1)S(1)} fusion(bf16[4,1,4,256,256]{3,4,2,0,1:T(8,128)(2,1)} %copy-done.1, bf16[16,1,4,256,256]{3,4,2,0,1:T(8,128)(2,1)} %bitcast.174, bf16[4,1,4,256,256]{3,4,2,0,1:T(8,128)(2,1)} %collective-permute-done), kind=kLoop, calls=%fused_computation.37 | loop fusion | flops 12582912 | bytes 25165824 | tf_op jit(solution)/shard_map/concatenate | solution.py:20
  164.6 20.0 %fusion.29 = bf16[16,1,4,256,256]{3,4,2,1,0:T(8,128)(2,1)} fusion(bf16[24,1,4,256,256]{3,4,2,0,1:T(8,128)(2,1)S(1)} %pad_maximum_fusion, s32[]{:T(128)S(6)} %select_n.47, f32[4]{0:T(128)S(1)} %get-tuple-element.136, s32[]{:T(128)S(6)} %select_n.46, f32[4]{0:T(128)S(1)} %get-tuple-element.135, f32[]{:T(128)} %bitcast.51, s32[]{:T(128)S(6)} %select_n.45, ...), kind=kLoop, calls=%fused_computation.38 | loop fusion | flops 121634816 | bytes 75563184 | tf_op jit(solution)/shard_map/convert_element_type | solution.py:85
  184.6 4.7 all-to-all-start.1
  191.2 142.2 %all-gather.2.cloned.1.call-done = bf16[16,256,256]{2,1,0:T(8,128)(2,1)} async-done(((bf16[1,256,256]{2,1,0:T(8,128)(2,1)}), bf16[16,256,256]{2,1,0:T(8,128)(2,1)}) %all-gather.2.cloned.1.call-update) | async-done | bytes 2097168 | tf_op jit(solution)/shard_map/all_gather | solution.py:87
  333.4 6.0 %all-to-all-done.1 = bf16[16,1,4,256,256]{3,4,2,1,0:T(8,128)(2,1)} async-done(((bf16[16,1,4,256,256]{3,4,2,1,0:T(8,128)(2,1)}), bf16[16,1,4,256,256]{3,4,2,1,0:T(8,128)(2,1)}, u32[]{:S(2)}, u32[]{:S(2)}) %all-to-all-start.1) | async-done | bytes 8388640 | tf_op jit(solution)/shard_map/all_to_all | solution.py:86
  339.3 92.7 %while.15 = (s32[]{:T(128)}, bf16[1,4,256,256]{3,2,1,0:T(8,128)(2,1)S(1)}, bf16[1,16,4,256,256]{4,3,2,1,0:T(8,128)(2,1)}, bf16[1,16,4,256,256]{3,4,2,1,0:T(8,128...) while((s32[]{:T(128)}, ...), condition=%wide.region_1.2_spmd, body=%wide.region_0.1_spmd.sunk | while | flops 807665664 | bytes 13895261 | solution.py:101
  346.1 1.7 fusion.67
  351.9 1.7 fusion.67
  357.7 1.7 fusion.67
  369.3 1.7 fusion.67
  375.1 1.7 fusion.67
  380.9 1.7 fusion.67
  386.7 1.7 fusion.67
  398.3 1.7 fusion.67
  404.0 1.7 fusion.67
  432.0 112.4 %all_to_all.40 = bf16[1,16,4,256,256]{4,3,2,0,1:T(8,128)(2,1)} all-to-all(bf16[1,16,4,256,256]{4,3,2,0,1:T(8,128)(2,1)} %bitcast.176), channel_id=1, replica_groups=mesh['energy'=8,'layer'=16] {'layer'}, dimensions={1} | all-to-all | bytes 16777216 | tf_op jit(solution)/shard_map/all_to_all | solution.py:104
  544.4 7.8 %copy.49 = bf16[16,1,4,256,256]{4,3,2,1,0:T(8,128)(2,1)} copy(bf16[16,1,4,256,256]{4,3,2,1,0:T(8,128)(2,1)} %bitcast.175) | data formatting | bytes 16777216
  (220 shorter events, 82.8 us)
Async XLA Ops:
  18.8 114.2 %copy-start.2 = (s32[4]{0:T(128)S(1)}, s32[4]{0:T(128)}, u32[]{:S(2)}) copy-start(s32[4]{0:T(128)} %param.11) | copy-start | bytes 52
  18.8 128.8 %copy-start.3 = (f32[4]{0:T(128)S(1)}, f32[4]{0:T(128)}, u32[]{:S(2)}) copy-start(f32[4]{0:T(128)} %param.12) | copy-start | bytes 52
  123.1 4.0 copy-start
  128.6 25.8 %collective-permute-start.1 = (bf16[4,1,4,256,256]{3,4,2,0,1:T(8,128)(2,1)}, bf16[4,1,4,256,256]{3,4,2,0,1:T(8,128)(2,1)S(1)}, u32[]{:S(2)}, u32[]{:S(2)}) collective-permute-start(bf16[4,1,4,256,256]{3,4,2,0,1:T(8,128)(2,1)} %slice_bitcast_fusion.10), channel_id=1, source_target_pairs={{16,0},{32,16},{48,32},{64,48},{80,64},{96,80},{112,96},{17,1},{33... | collective-permute-start | bytes 6291464 | tf_op jit(solution)/shard_map/ppermute | solution.py:19
  130.6 27.7 %collective-permute-start = (bf16[4,1,4,256,256]{3,4,2,0,1:T(8,128)(2,1)}, bf16[4,1,4,256,256]{3,4,2,0,1:T(8,128)(2,1)}, u32[]{:S(2)}, u32[]{:S(2)}) collective-permute-start(bf16[4,1,4,256,256]{3,4,2,0,1:T(8,128)(2,1)} %slice_bitcast_fusion.11), channel_id=1, source_target_pairs={{0,16},{16,32},{32,48},{48,64},{64,80},{80,96},{96,112},{1,17},{17... | collective-permute-start | bytes 6291464 | tf_op jit(solution)/shard_map/ppermute | solution.py:16
  154.4 3.8 copy-start.1
  184.6 154.7 %all-to-all-start.1 = ((bf16[16,1,4,256,256]{3,4,2,1,0:T(8,128)(2,1)}), bf16[16,1,4,256,256]{3,4,2,1,0:T(8,128)(2,1)}, u32[]{:S(2)}, u32[]{:S(2)}) async-start(bf16[16,1,4,256,256]{3,4,2,1,0:T(8,128)(2,1)} %fusion.29), calls=%async_computation.1 | async-start | bytes 16777216 | tf_op jit(solution)/shard_map/all_to_all | solution.py:86
  189.4 144.0 %all-gather.2.cloned.1.call-start = ((), (), s32[]{:S(2)}) async-start(), calls=%async_computation.3 | async-start | bytes 2228224 | tf_op jit(solution)/shard_map/all_gather | solution.py:87
Sparse Core Ops, SparseCore 0:
  192.3 140.9 all-gather.1
where the time goes:
time: 561 us; the launch traced here: 559 us
  blocking collectives  217 us (39%)
  waiting for transfers between devices  159 us (28%)
  matrix products  61.4 us (11%)
  local copies, waits for them, and re-layouts  57.3 us (10%)
  other arithmetic  27.6 us (5%)
  between operations  27 us (5%)
  starting transfers between devices  9.1 us (2%)
    all_gather x1, waiting for transfers between devices, body(): couplings = lax.all_gather(coupling, 'layer', axis=0, tiled=True)  142 us
    all_to_all x1, blocking collectives, body(): lax.all_to_all(finished, 'layer', split_axis=1, concat_axis=0, tiled=True)  112 us
    all_to_all x1, blocking collectives, body(): lax.all_to_all(correlations, 'layer', split_axis=1, concat_axis=0, tiled=...  104 us
    dot_general x16, matrix products, advance(): jnp.einsum('ab,...kbc->...kac', coupling_block, halfway, preferred_elemen...  27.3 us
    unnamed x10, local copies, waits for them, and re-layouts  22.5 us
    convert_element_type x1, other arithmetic, body(): sigma_blocks = jnp.where(live_mask, accumulated, 0.0).astype(jnp.bfloat16)  20 us
    dot_general x64, matrix products, right_product(): jnp.einsum('...kab,...cb->...kac', stacked_block, matrix, preferred_eleme...  17.5 us
    dot_general x64, matrix products, left_product(): jnp.einsum('...ab,...kbc->...kac', matrix, stacked_block, preferred_eleme...  16.5 us
  transfers between devices with their start and end apart: 4, of which 4 were waited for; matrix products, arithmetic and copies ran while one was open for 1% of the time, Pallas kernels for 0%

commit v1 on v0

--- a/solution.py
+++ b/solution.py
@@ -6,6 +6,18 @@
 MODES = 4
 SHIFT_MAX = 4
 bose_ratio = 0.5
+
+
+def object_refer(message, join_dim):
+    degree = lax.axis_size("layer")
+    by_place = [(s, (s + 1) % degree) for s in range(degree)]
+    seen_now = [None] * degree
+    seen_now[degree - 1] = message
+    for dev_j in range(degree - 2, -1, -1):
+        seen_now[dev_j] = lax.ppermute(seen_now[dev_j + 1], axis_name="layer", perm=by_place)
+    arr_now = jnp.concatenate(seen_now, axis=join_dim)
+    v_next = (lax.axis_index("layer") + 1) * message.shape[join_dim]
+    return jnp.roll(arr_now, v_next, axis=join_dim)
 
 
 def with_halo(block, sides, width):
@@ -84,7 +96,7 @@
     live_mask = (orbital_index[:, None] < live_count) & (orbital_index[None, :] < live_count)
     sigma_blocks = jnp.where(live_mask, accumulated, 0.0).astype(jnp.bfloat16)
     returned = lax.all_to_all(sigma_blocks, "layer", split_axis=0, concat_axis=1, tiled=True)
-    couplings = lax.all_gather(coupling, "layer", axis=0, tiled=True)
+    couplings = object_refer(coupling, 0)
     layer_total = returned.shape[1]
 
     def layer_step(layer_index, state):

time: 561 us -> 600 us (1.070)
  waiting for transfers between devices: 159 us -> 223 us
  blocking collectives: 217 us -> 197 us
  between operations: 27 us -> 13.4 us
  starting transfers between devices: 9.1 us -> 19.9 us
    ppermute x0 -> x15, waiting for transfers between devices: none -> 212 us  [object_refer(): lax.ppermute(seen_now[dev_j + 1], axis_name='layer', perm=by_place)]
    all_gather x1 -> x0, waiting for transfers between devices: 142 us -> none  [body(): couplings = lax.all_gather(coupling, 'layer', axis=0, tiled=True)]
    all_to_all x1, blocking collectives: 112 us -> 92.3 us  [body(): lax.all_to_all(finished, 'layer', split_axis=1, concat_axis=0, tiled=True)]
    ppermute x0 -> x15, starting transfers between devices: none -> 10.7 us  [object_refer(): lax.ppermute(seen_now[dev_j + 1], axis_name='layer', perm=by_place)]
    unnamed x10 -> x43, local copies, waits for them, and re-layouts: 22.5 us -> 21.4 us
  transfers between devices with their start and end apart: 4 -> 18, of which waited for: 4 -> 17; matrix products, arithmetic and copies ran while one was open for 1% -> 1% of each run, Pallas kernels for 0% -> 0%
where the time goes in v1:
time: 600 us; the launch traced here: 598 us
  waiting for transfers between devices  223 us (37%)
  blocking collectives  197 us (33%)
  matrix products  59.2 us (10%)
  local copies, waits for them, and re-layouts  56.9 us (9%)
  other arithmetic  27.8 us (5%)
  starting transfers between devices  19.9 us (3%)
  between operations  13.4 us (2%)
    ppermute x15, waiting for transfers between devices, object_refer(): lax.ppermute(seen_now[dev_j + 1], axis_name='layer', perm=by_place)  212 us
    all_to_all x1, blocking collectives, body(): lax.all_to_all(correlations, 'layer', split_axis=1, concat_axis=0, tiled=...  104 us
    all_to_all x1, blocking collectives, body(): lax.all_to_all(finished, 'layer', split_axis=1, concat_axis=0, tiled=True)  92.3 us
    dot_general x16, matrix products, advance(): jnp.einsum('ab,...kbc->...kac', coupling_block, halfway, preferred_elemen...  25 us
    unnamed x43, local copies, waits for them, and re-layouts  21.4 us
    convert_element_type x1, other arithmetic, body(): sigma_blocks = jnp.where(live_mask, accumulated, 0.0).astype(jnp.bfloat16)  20.2 us
    dot_general x64, matrix products, right_product(): jnp.einsum('...kab,...cb->...kac', stacked_block, matrix, preferred_eleme...  17.5 us
    dot_general x64, matrix products, left_product(): jnp.einsum('...ab,...kbc->...kac', matrix, stacked_block, preferred_eleme...  16.6 us
  transfers between devices with their start and end apart: 18, of which 17 were waited for; matrix products, arithmetic and copies ran while one was open for 1% of the time, Pallas kernels for 0%

profile of v1, /device:TPU:8, one launch (start us, length us, event | category | flops | bytes accessed | tf_op | source)
XLA Modules:
  0.0 597.7 jit_solution(4149869393702816642)
XLA Ops:
  0.0 12.2 %copy.25 = bf16[1,16,4,256,256]{3,4,2,0,1:T(8,128)(2,1)} copy(bf16[1,16,4,256,256]{4,3,2,1,0:T(8,128)(2,1)} %param.8) | data formatting | bytes 16777216 | tf_op args[0]
  12.2 104.2 %all_to_all.39 = bf16[1,16,4,256,256]{3,4,2,0,1:T(8,128)(2,1)S(1)} all-to-all(bf16[1,16,4,256,256]{3,4,2,0,1:T(8,128)(2,1)} %copy.25), channel_id=1, replica_groups=mesh['energy'=8,'layer'=16] {'layer'}, dimensions={1} | all-to-all | bytes 16777216 | tf_op jit(solution)/shard_map/all_to_all | solution.py:80
  140.2 6.6 %collective-permute-done.1 = bf16[4,1,4,256,256]{3,4,2,0,1:T(8,128)(2,1)S(1)} collective-permute-done((bf16[4,1,4,256,256]{3,4,2,0,1:T(8,128)(2,1)}, bf16[4,1,4,256,256]{3,4,2,0,1:T(8,128)(2,1)S(1)}, u32[]{:S(2)}, u32[]{:S(2)}) %collective-permute-start.1) | collective-permute-done | bytes 2097184 | tf_op jit(solution)/shard_map/ppermute | solution.py:31
  150.7 6.4 %pad_maximum_fusion = bf16[24,1,4,256,256]{3,4,2,0,1:T(8,128)(2,1)S(1)} fusion(bf16[4,1,4,256,256]{3,4,2,0,1:T(8,128)(2,1)} %copy-done.1, bf16[16,1,4,256,256]{3,4,2,0,1:T(8,128)(2,1)} %bitcast.174, bf16[4,1,4,256,256]{3,4,2,0,1:T(8,128)(2,1)} %collective-permute-done), kind=kLoop, calls=%fused_computation.37 | loop fusion | flops 12582912 | bytes 25165824 | tf_op jit(solution)/shard_map/concatenate | solution.py:32
  157.1 20.2 %fusion.29 = bf16[16,1,4,256,256]{3,4,2,1,0:T(8,128)(2,1)} fusion(bf16[24,1,4,256,256]{3,4,2,0,1:T(8,128)(2,1)S(1)} %pad_maximum_fusion, s32[]{:T(128)S(6)} %select_n.60, f32[4]{0:T(128)S(1)} %get-tuple-element.136, s32[]{:T(128)S(6)} %select_n.59, f32[4]{0:T(128)S(1)} %get-tuple-element.135, f32[]{:T(128)} %bitcast.51, s32[]{:T(128)S(6)} %select_n.58, ...), kind=kLoop, calls=%fused_computation.38 | loop fusion | flops 121634816 | bytes 75563184 | tf_op jit(solution)/shard_map/convert_element_type | solution.py:97
  177.2 4.9 all-to-all-start.1
  184.0 103.0 %collective-permute-done.2 = bf16[1,256,256]{2,1,0:T(8,128)(2,1)S(1)} collective-permute-done((bf16[1,256,256]{2,1,0:T(8,128)(2,1)S(1)}, bf16[1,256,256]{2,1,0:T(8,128)(2,1)S(1)}, u32[]{:S(2)}, u32[]{:S(2)}) %collective-permute-start.2) | collective-permute-done | bytes 131104 | tf_op jit(solution)/shard_map/ppermute | solution.py:17
  287.0 8.3 %collective-permute-done.3 = bf16[1,256,256]{2,1,0:T(8,128)(2,1)S(1)} collective-permute-done((bf16[1,256,256]{2,1,0:T(8,128)(2,1)S(1)}, bf16[1,256,256]{2,1,0:T(8,128)(2,1)S(1)}, u32[]{:S(2)}, u32[]{:S(2)}) %collective-permute-start.3) | collective-permute-done | bytes 131104 | tf_op jit(solution)/shard_map/ppermute | solution.py:17
  295.2 9.1 %collective-permute-done.4 = bf16[1,256,256]{2,1,0:T(8,128)(2,1)S(1)} collective-permute-done((bf16[1,256,256]{2,1,0:T(8,128)(2,1)S(1)}, bf16[1,256,256]{2,1,0:T(8,128)(2,1)S(1)}, u32[]{:S(2)}, u32[]{:S(2)}) %collective-permute-start.4) | collective-permute-done | bytes 131104 | tf_op jit(solution)/shard_map/ppermute | solution.py:17
  306.9 6.3 %collective-permute-done.5 = bf16[1,256,256]{2,1,0:T(8,128)(2,1)S(1)} collective-permute-done((bf16[1,256,256]{2,1,0:T(8,128)(2,1)S(1)}, bf16[1,256,256]{2,1,0:T(8,128)(2,1)S(1)}, u32[]{:S(2)}, u32[]{:S(2)}) %collective-permute-start.5) | collective-permute-done | bytes 131104 | tf_op jit(solution)/shard_map/ppermute | solution.py:17
  313.1 4.6 collective-permute-start.6
  323.2 6.5 %collective-permute-done.7 = bf16[1,256,256]{2,1,0:T(8,128)(2,1)S(1)} collective-permute-done((bf16[1,256,256]{2,1,0:T(8,128)(2,1)S(1)}, bf16[1,256,256]{2,1,0:T(8,128)(2,1)S(1)}, u32[]{:S(2)}, u32[]{:S(2)}) %collective-permute-start.7) | collective-permute-done | bytes 131104 | tf_op jit(solution)/shard_map/ppermute | solution.py:17
  329.7 8.3 %collective-permute-done.8 = bf16[1,256,256]{2,1,0:T(8,128)(2,1)S(1)} collective-permute-done((bf16[1,256,256]{2,1,0:T(8,128)(2,1)S(1)}, bf16[1,256,256]{2,1,0:T(8,128)(2,1)S(1)}, u32[]{:S(2)}, u32[]{:S(2)}) %collective-permute-start.8) | collective-permute-done | bytes 131104 | tf_op jit(solution)/shard_map/ppermute | solution.py:17
  338.0 8.3 %collective-permute-done.9 = bf16[1,256,256]{2,1,0:T(8,128)(2,1)S(1)} collective-permute-done((bf16[1,256,256]{2,1,0:T(8,128)(2,1)S(1)}, bf16[1,256,256]{2,1,0:T(8,128)(2,1)S(1)}, u32[]{:S(2)}, u32[]{:S(2)}) %collective-permute-start.9) | collective-permute-done | bytes 131104 | tf_op jit(solution)/shard_map/ppermute | solution.py:17
  346.3 8.3 %collective-permute-done.10 = bf16[1,256,256]{2,1,0:T(8,128)(2,1)S(1)} collective-permute-done((bf16[1,256,256]{2,1,0:T(8,128)(2,1)S(1)}, bf16[1,256,256]{2,1,0:T(8,128)(2,1)S(1)}, u32[]{:S(2)}, u32[]{:S(2)}) %collective-permute-start.10) | collective-permute-done | bytes 131104 | tf_op jit(solution)/shard_map/ppermute | solution.py:17
  354.6 8.3 %collective-permute-done.11 = bf16[1,256,256]{2,1,0:T(8,128)(2,1)S(1)} collective-permute-done((bf16[1,256,256]{2,1,0:T(8,128)(2,1)S(1)}, bf16[1,256,256]{2,1,0:T(8,128)(2,1)S(1)}, u32[]{:S(2)}, u32[]{:S(2)}) %collective-permute-start.11) | collective-permute-done | bytes 131104 | tf_op jit(solution)/shard_map/ppermute | solution.py:17
  362.9 8.4 %collective-permute-done.12 = bf16[1,256,256]{2,1,0:T(8,128)(2,1)S(1)} collective-permute-done((bf16[1,256,256]{2,1,0:T(8,128)(2,1)S(1)}, bf16[1,256,256]{2,1,0:T(8,128)(2,1)S(1)}, u32[]{:S(2)}, u32[]{:S(2)}) %collective-permute-start.12) | collective-permute-done | bytes 131104 | tf_op jit(solution)/shard_map/ppermute | solution.py:17
  371.3 9.6 %collective-permute-done.13 = bf16[1,256,256]{2,1,0:T(8,128)(2,1)S(1)} collective-permute-done((bf16[1,256,256]{2,1,0:T(8,128)(2,1)S(1)}, bf16[1,256,256]{2,1,0:T(8,128)(2,1)S(1)}, u32[]{:S(2)}, u32[]{:S(2)}) %collective-permute-start.13) | collective-permute-done | bytes 131104 | tf_op jit(solution)/shard_map/ppermute | solution.py:17
  380.8 8.8 %collective-permute-done.14 = bf16[1,256,256]{2,1,0:T(8,128)(2,1)S(1)} collective-permute-done((bf16[1,256,256]{2,1,0:T(8,128)(2,1)S(1)}, bf16[1,256,256]{2,1,0:T(8,128)(2,1)S(1)}, u32[]{:S(2)}, u32[]{:S(2)}) %collective-permute-start.14) | collective-permute-done | bytes 131104 | tf_op jit(solution)/shard_map/ppermute | solution.py:17
  389.7 8.3 %collective-permute-done.15 = bf16[1,256,256]{2,1,0:T(8,128)(2,1)S(1)} collective-permute-done((bf16[1,256,256]{2,1,0:T(8,128)(2,1)S(1)}, bf16[1,256,256]{2,1,0:T(8,128)(2,1)S(1)}, u32[]{:S(2)}, u32[]{:S(2)}) %collective-permute-start.15) | collective-permute-done | bytes 131104 | tf_op jit(solution)/shard_map/ppermute | solution.py:17
  399.0 7.2 %collective-permute-done.16 = bf16[1,256,256]{2,1,0:T(8,128)(2,1)S(1)} collective-permute-done((bf16[1,256,256]{2,1,0:T(8,128)(2,1)S(1)}, bf16[1,256,256]{2,1,0:T(8,128)(2,1)S(1)}, u32[]{:S(2)}, u32[]{:S(2)}) %collective-permute-start.16) | collective-permute-done | bytes 131104 | tf_op jit(solution)/shard_map/ppermute | solution.py:17
  407.0 90.6 %while.15 = (s32[]{:T(128)}, bf16[1,4,256,256]{3,2,1,0:T(8,128)(2,1)S(1)}, bf16[1,16,4,256,256]{4,3,2,1,0:T(8,128)(2,1)}, bf16[1,16,4,256,256]{3,4,2,1,0:T(8,128...) while((s32[]{:T(128)}, ...), condition=%wide.region_1.2_spmd, body=%wide.region_0.1_spmd.sunk | while | flops 807665664 | bytes 13895261 | solution.py:113
  497.6 92.3 %all_to_all.40 = bf16[1,16,4,256,256]{4,3,2,0,1:T(8,128)(2,1)} all-to-all(bf16[1,16,4,256,256]{4,3,2,0,1:T(8,128)(2,1)} %bitcast.176), channel_id=1, replica_groups=mesh['energy'=8,'layer'=16] {'layer'}, dimensions={1} | all-to-all | bytes 16777216 | tf_op jit(solution)/shard_map/all_to_all | solution.py:116
  589.9 7.8 %copy.80 = bf16[16,1,4,256,256]{4,3,2,1,0:T(8,128)(2,1)} copy(bf16[16,1,4,256,256]{4,3,2,1,0:T(8,128)(2,1)} %bitcast.175) | data formatting | bytes 16777216
  (282 shorter events, 115.3 us)
Async XLA Ops:
  116.4 4.7 copy-start
  116.4 9.0 %copy-start.3 = (s32[4]{0:T(128)S(1)}, s32[4]{0:T(128)}, u32[]{:S(2)}) copy-start(s32[4]{0:T(128)} %param.11) | copy-start | bytes 52
  116.4 23.0 %copy-start.4 = (f32[4]{0:T(128)S(1)}, f32[4]{0:T(128)}, u32[]{:S(2)}) copy-start(f32[4]{0:T(128)} %param.12) | copy-start | bytes 52
  121.1 25.8 %collective-permute-start.1 = (bf16[4,1,4,256,256]{3,4,2,0,1:T(8,128)(2,1)}, bf16[4,1,4,256,256]{3,4,2,0,1:T(8,128)(2,1)S(1)}, u32[]{:S(2)}, u32[]{:S(2)}) collective-permute-start(bf16[4,1,4,256,256]{3,4,2,0,1:T(8,128)(2,1)} %slice_bitcast_fusion.10), channel_id=1, source_target_pairs={{16,0},{32,16},{48,32},{64,48},{80,64},{96,80},{112,96},{17,1},{33... | collective-permute-start | bytes 6291464 | tf_op jit(solution)/shard_map/ppermute | solution.py:31
  123.0 27.7 %collective-permute-start = (bf16[4,1,4,256,256]{3,4,2,0,1:T(8,128)(2,1)}, bf16[4,1,4,256,256]{3,4,2,0,1:T(8,128)(2,1)}, u32[]{:S(2)}, u32[]{:S(2)}) collective-permute-start(bf16[4,1,4,256,256]{3,4,2,0,1:T(8,128)(2,1)} %slice_bitcast_fusion.11), channel_id=1, source_target_pairs={{0,16},{16,32},{32,48},{48,64},{64,80},{80,96},{96,112},{1,17},{17... | collective-permute-start | bytes 6291464 | tf_op jit(solution)/shard_map/ppermute | solution.py:28
  146.9 3.8 copy-start.1
  177.2 4.9 copy-start.2
  177.2 229.8 %all-to-all-start.1 = ((bf16[16,1,4,256,256]{3,4,2,1,0:T(8,128)(2,1)}), bf16[16,1,4,256,256]{3,4,2,1,0:T(8,128)(2,1)}, u32[]{:S(2)}, u32[]{:S(2)}) async-start(bf16[16,1,4,256,256]{3,4,2,1,0:T(8,128)(2,1)} %fusion.29), calls=%async_computation.1 | async-start | bytes 16777216 | tf_op jit(solution)/shard_map/all_to_all | solution.py:98
  182.2 104.8 %collective-permute-start.2 = (bf16[1,256,256]{2,1,0:T(8,128)(2,1)S(1)}, bf16[1,256,256]{2,1,0:T(8,128)(2,1)S(1)}, u32[]{:S(2)}, u32[]{:S(2)}) collective-permute-start(bf16[1,256,256]{2,1,0:T(8,128)(2,1)S(1)} %copy-done.2), channel_id=1, source_target_pairs={{0,1},{1,2},{2,3},{3,4},{4,5},{5,6},{6,7},{7,8},{8,9},{9,10},{10,1... | collective-permute-start | bytes 393224 | tf_op jit(solution)/shard_map/ppermute | solution.py:17
  287.0 8.3 %collective-permute-start.3 = (bf16[1,256,256]{2,1,0:T(8,128)(2,1)S(1)}, bf16[1,256,256]{2,1,0:T(8,128)(2,1)S(1)}, u32[]{:S(2)}, u32[]{:S(2)}) collective-permute-start(bf16[1,256,256]{2,1,0:T(8,128)(2,1)S(1)} %collective-permute-done.2), channel_id=1, source_target_pairs={{0,1},{1,2},{2,3},{3,4},{4,5},{5,6},{6,7},{7,8},{8,9},{9,10},{10,1... | collective-permute-start | bytes 393224 | tf_op jit(solution)/shard_map/ppermute | solution.py:17
  295.2 9.1 %collective-permute-start.4 = (bf16[1,256,256]{2,1,0:T(8,128)(2,1)S(1)}, bf16[1,256,256]{2,1,0:T(8,128)(2,1)S(1)}, u32[]{:S(2)}, u32[]{:S(2)}) collective-permute-start(bf16[1,256,256]{2,1,0:T(8,128)(2,1)S(1)} %collective-permute-done.3), channel_id=1, source_target_pairs={{0,1},{1,2},{2,3},{3,4},{4,5},{5,6},{6,7},{7,8},{8,9},{9,10},{10,1... | collective-permute-start | bytes 393224 | tf_op jit(solution)/shard_map/ppermute | solution.py:17
  304.4 8.7 %collective-permute-start.5 = (bf16[1,256,256]{2,1,0:T(8,128)(2,1)S(1)}, bf16[1,256,256]{2,1,0:T(8,128)(2,1)S(1)}, u32[]{:S(2)}, u32[]{:S(2)}) collective-permute-start(bf16[1,256,256]{2,1,0:T(8,128)(2,1)S(1)} %collective-permute-done.4), channel_id=1, source_target_pairs={{0,1},{1,2},{2,3},{3,4},{4,5},{5,6},{6,7},{7,8},{8,9},{9,10},{10,1... | collective-permute-start | bytes 393224 | tf_op jit(solution)/shard_map/ppermute | solution.py:17
  313.1 8.3 %collective-permute-start.6 = (bf16[1,256,256]{2,1,0:T(8,128)(2,1)S(1)}, bf16[1,256,256]{2,1,0:T(8,128)(2,1)S(1)}, u32[]{:S(2)}, u32[]{:S(2)}) collective-permute-start(bf16[1,256,256]{2,1,0:T(8,128)(2,1)S(1)} %collective-permute-done.5), channel_id=1, source_target_pairs={{0,1},{1,2},{2,3},{3,4},{4,5},{5,6},{6,7},{7,8},{8,9},{9,10},{10,1... | collective-permute-start | bytes 393224 | tf_op jit(solution)/shard_map/ppermute | solution.py:17
  321.4 8.3 %collective-permute-start.7 = (bf16[1,256,256]{2,1,0:T(8,128)(2,1)S(1)}, bf16[1,256,256]{2,1,0:T(8,128)(2,1)S(1)}, u32[]{:S(2)}, u32[]{:S(2)}) collective-permute-start(bf16[1,256,256]{2,1,0:T(8,128)(2,1)S(1)} %collective-permute-done.6), channel_id=1, source_target_pairs={{0,1},{1,2},{2,3},{3,4},{4,5},{5,6},{6,7},{7,8},{8,9},{9,10},{10,1... | collective-permute-start | bytes 393224 | tf_op jit(solution)/shard_map/ppermute | solution.py:17
  329.7 8.3 %collective-permute-start.8 = (bf16[1,256,256]{2,1,0:T(8,128)(2,1)S(1)}, bf16[1,256,256]{2,1,0:T(8,128)(2,1)S(1)}, u32[]{:S(2)}, u32[]{:S(2)}) collective-permute-start(bf16[1,256,256]{2,1,0:T(8,128)(2,1)S(1)} %collective-permute-done.7), channel_id=1, source_target_pairs={{0,1},{1,2},{2,3},{3,4},{4,5},{5,6},{6,7},{7,8},{8,9},{9,10},{10,1... | collective-permute-start | bytes 393224 | tf_op jit(solution)/shard_map/ppermute | solution.py:17
  338.0 8.3 %collective-permute-start.9 = (bf16[1,256,256]{2,1,0:T(8,128)(2,1)S(1)}, bf16[1,256,256]{2,1,0:T(8,128)(2,1)S(1)}, u32[]{:S(2)}, u32[]{:S(2)}) collective-permute-start(bf16[1,256,256]{2,1,0:T(8,128)(2,1)S(1)} %collective-permute-done.8), channel_id=1, source_target_pairs={{0,1},{1,2},{2,3},{3,4},{4,5},{5,6},{6,7},{7,8},{8,9},{9,10},{10,1... | collective-permute-start | bytes 393224 | tf_op jit(solution)/shard_map/ppermute | solution.py:17
  346.3 8.3 %collective-permute-start.10 = (bf16[1,256,256]{2,1,0:T(8,128)(2,1)S(1)}, bf16[1,256,256]{2,1,0:T(8,128)(2,1)S(1)}, u32[]{:S(2)}, u32[]{:S(2)}) collective-permute-start(bf16[1,256,256]{2,1,0:T(8,128)(2,1)S(1)} %collective-permute-done.9), channel_id=1, source_target_pairs={{0,1},{1,2},{2,3},{3,4},{4,5},{5,6},{6,7},{7,8},{8,9},{9,10},{10,1... | collective-permute-start | bytes 393224 | tf_op jit(solution)/shard_map/ppermute | solution.py:17
  354.6 8.3 %collective-permute-start.11 = (bf16[1,256,256]{2,1,0:T(8,128)(2,1)S(1)}, bf16[1,256,256]{2,1,0:T(8,128)(2,1)S(1)}, u32[]{:S(2)}, u32[]{:S(2)}) collective-permute-start(bf16[1,256,256]{2,1,0:T(8,128)(2,1)S(1)} %collective-permute-done.10), channel_id=1, source_target_pairs={{0,1},{1,2},{2,3},{3,4},{4,5},{5,6},{6,7},{7,8},{8,9},{9,10},{10,1... | collective-permute-start | bytes 393224 | tf_op jit(solution)/shard_map/ppermute | solution.py:17
  362.8 8.4 %collective-permute-start.12 = (bf16[1,256,256]{2,1,0:T(8,128)(2,1)S(1)}, bf16[1,256,256]{2,1,0:T(8,128)(2,1)S(1)}, u32[]{:S(2)}, u32[]{:S(2)}) collective-permute-start(bf16[1,256,256]{2,1,0:T(8,128)(2,1)S(1)} %collective-permute-done.11), channel_id=1, source_target_pairs={{0,1},{1,2},{2,3},{3,4},{4,5},{5,6},{6,7},{7,8},{8,9},{9,10},{10,1... | collective-permute-start | bytes 393224 | tf_op jit(solution)/shard_map/ppermute | solution.py:17
  371.3 9.6 %collective-permute-start.13 = (bf16[1,256,256]{2,1,0:T(8,128)(2,1)S(1)}, bf16[1,256,256]{2,1,0:T(8,128)(2,1)S(1)}, u32[]{:S(2)}, u32[]{:S(2)}) collective-permute-start(bf16[1,256,256]{2,1,0:T(8,128)(2,1)S(1)} %collective-permute-done.12), channel_id=1, source_target_pairs={{0,1},{1,2},{2,3},{3,4},{4,5},{5,6},{6,7},{7,8},{8,9},{9,10},{10,1... | collective-permute-start | bytes 393224 | tf_op jit(solution)/shard_map/ppermute | solution.py:17
  380.8 8.8 %collective-permute-start.14 = (bf16[1,256,256]{2,1,0:T(8,128)(2,1)S(1)}, bf16[1,256,256]{2,1,0:T(8,128)(2,1)S(1)}, u32[]{:S(2)}, u32[]{:S(2)}) collective-permute-start(bf16[1,256,256]{2,1,0:T(8,128)(2,1)S(1)} %collective-permute-done.13), channel_id=1, source_target_pairs={{0,1},{1,2},{2,3},{3,4},{4,5},{5,6},{6,7},{7,8},{8,9},{9,10},{10,1... | collective-permute-start | bytes 393224 | tf_op jit(solution)/shard_map/ppermute | solution.py:17
  389.6 8.3 %collective-permute-start.15 = (bf16[1,256,256]{2,1,0:T(8,128)(2,1)S(1)}, bf16[1,256,256]{2,1,0:T(8,128)(2,1)S(1)}, u32[]{:S(2)}, u32[]{:S(2)}) collective-permute-start(bf16[1,256,256]{2,1,0:T(8,128)(2,1)S(1)} %collective-permute-done.14), channel_id=1, source_target_pairs={{0,1},{1,2},{2,3},{3,4},{4,5},{5,6},{6,7},{7,8},{8,9},{9,10},{10,1... | collective-permute-start | bytes 393224 | tf_op jit(solution)/shard_map/ppermute | solution.py:17
  397.9 8.3 %collective-permute-start.16 = (bf16[1,256,256]{2,1,0:T(8,128)(2,1)S(1)}, bf16[1,256,256]{2,1,0:T(8,128)(2,1)S(1)}, u32[]{:S(2)}, u32[]{:S(2)}) collective-permute-start(bf16[1,256,256]{2,1,0:T(8,128)(2,1)S(1)} %collective-permute-done.15), channel_id=1, source_target_pairs={{0,1},{1,2},{2,3},{3,4},{4,5},{5,6},{6,7},{7,8},{8,9},{9,10},{10,1... | collective-permute-start | bytes 393224 | tf_op jit(solution)/shard_map/ppermute | solution.py:17
